TPU v7x, 32 devices: a whole 2x2x4 slice. The times are simulated.
32 devices in a mesh: row: 4 (over y, x), col: 8 (over z, core).
Axes of the slice: x: 2, y: 2, z: 4, core: 2. Of those that a mesh axis runs over, the one named last changes fastest.
Arguments:
- query_act: bfloat16 [768, 16384], P(None, 'row'), may hold values from -6 to 6
- query_grad: bfloat16 [768, 16384], P(None, 'col'), may hold values from -6 to 6
- train_rot: bfloat16 [384, 16384], P(None, 'col'), may hold values from -6 to 6
- basis_in: bfloat16 [16384, 16384], P('row', 'col'), may hold values from -0.046875 to 0.046875
- basis_out: bfloat16 [16384, 16384], P('col', 'row'), may hold values from -0.046875 to 0.046875
- eig_in: float32 [16384], replicated, may hold values from 0.05 to 2
- eig_out: float32 [16384], replicated, may hold values from 0.05 to 2
Outputs:
- predicted: float32 [384, 16384], P('row', 'col')
All inputs are finite; a program needn't handle non-finite values.
Results may differ from a plain program's by a relative error of at most 0.0049.
Values may be sent and summed in bfloat16 or wider, within the bound.
A program may use at most 128 MiB of HBM per device.

v0:
```python
import functools

import jax
import jax.numpy as jnp
from jax import lax
from jax.experimental import pallas as pl
from jax.experimental.pallas import tpu as pltpu
from jax.sharding import PartitionSpec as P

damping_share = 0.1
chunk_width = 256
act_every = 2
gather_lag = 5
stash_slots = 4
MESH = pl.DeviceIdType.MESH
f32 = jnp.float32
bf16 = jnp.bfloat16


def remote(src, dst, send, recv, device):
    return pltpu.make_async_remote_copy(
        src_ref=src, dst_ref=dst, send_sem=send, recv_sem=recv,
        device_id=device, device_id_type=MESH,
    )


class Line:
    def __init__(self, place, count, half, wire, bufs, sems, scale):
        self.place, self.count, self.half, self.wire, self.scale = place, count, half, wire, scale
        (self.pair_out, self.pair_in, self.stash, self.out, self.inward_in, self.across_in, self.full) = bufs
        (self.pair_s, self.pair_r, self.out_s, self.inward_r, self.across_r,
         self.back_s, self.back_r, self.mate_s, self.mate_r) = sems

    @staticmethod
    def buffers(count, half, width, wire):
        return [
            pltpu.VMEM((2, half, width), f32),
            pltpu.VMEM((2, half, width), f32),
            pltpu.VMEM((stash_slots, half, width), f32),
            pltpu.VMEM((2, half, width), wire),
            pltpu.VMEM((count, half, width), wire),
            pltpu.VMEM((count, half, width), wire),
            pltpu.VMEM((count, 2, half, width), bf16),
        ]

    @staticmethod
    def semaphores(count):
        dma = pltpu.SemaphoreType.DMA
        return [dma((2,)), dma((count,)), dma((2,)), dma((count,)), dma((count,)),
                dma((count,)), dma((count,)), dma((count,)), dma((count,))]

    def pair(self, k):
        slot = k % 2
        return remote(self.pair_out.at[slot], self.pair_in.at[slot], self.pair_s.at[slot],
                      self.pair_r.at[k], {"col": self.place.partner})

    def inward(self, k):
        slot = k % 2
        return remote(self.out.at[slot], self.inward_in.at[k], self.out_s.at[slot],
                      self.inward_r.at[k], {"col": self.place.inward})

    def across(self, k):
        slot = k % 2
        return remote(self.out.at[slot], self.across_in.at[k], self.out_s.at[slot],
                      self.across_r.at[k], {"col": self.place.inward})

    def back(self, k):
        piece = self.full.at[k, self.place.core]
        return remote(piece, piece, self.back_s.at[k], self.back_r.at[k], {"col": self.place.outward})

    def mate(self, k):
        piece = self.full.at[k, self.place.core]
        return remote(piece, piece, self.mate_s.at[k], self.mate_r.at[k], {"col": self.place.partner})

    def start(self, k, theirs, mine):
        @pl.when(k >= 2)
        def _():
            self.pair(k - 2).wait_send()
        self.pair_out[k % 2] = theirs()
        self.pair(k).start()
        self.stash[k % stash_slots] = mine()

    def send_out(self, k, total, first):
        @pl.when(k >= 2)
        def _():
            self.inward(k - 2).wait_send()
        self.out[k % 2] = total.astype(self.wire)
        if self.place.reach == 1:
            self.across(k).start()
        elif first:
            self.inward(k).start()
        else:
            @pl.when(self.place.middle)
            def _():
                self.across(k).start()
            @pl.when(jnp.logical_not(self.place.middle))
            def _():
                self.inward(k).start()

    def pair_sum(self, k):
        self.pair(k).wait_recv()
        slot = k % stash_slots
        total = self.stash[slot] + self.pair_in[k % 2]
        self.stash[slot] = total

        @pl.when(self.place.depth == 0)
        def _():
            self.send_out(k, total, True)

    def add_inward(self, k):
        if self.place.reach == 1:
            return

        @pl.when(self.place.depth > 0)
        def _():
            self.inward(k).wait_recv()
            slot = k % stash_slots
            total = self.stash[slot] + self.inward_in[k].astype(f32)
            self.stash[slot] = total
            self.send_out(k, total, False)

    def add_across(self, k):
        @pl.when(self.place.middle)
        def _():
            self.across(k).wait_recv()
            total = self.stash[k % stash_slots] + self.across_in[k].astype(f32)
            if self.scale is not None:
                total = total * self.scale
            self.full[k, self.place.core] = total.astype(bf16)
            if self.place.reach > 1:
                self.back(k).start()
            self.mate(k).start()

    def relay(self, k):
        if self.place.reach == 1:
            return

        @pl.when(jnp.logical_not(self.place.middle))
        def _():
            self.back(k).wait_recv()

            @pl.when(self.place.depth > 0)
            def _():
                self.back(k).start()
            self.mate(k).start()

    def ready(self, k):
        self.mate(k).wait_recv()
        self.mate(k).wait_send()
        if self.place.reach > 1:
            @pl.when(self.place.depth > 0)
            def _():
                self.back(k).wait_send()

    def drain(self):
        for k in range(max(0, self.count - 2), self.count):
            self.pair(k).wait_send()
            self.inward(k).wait_send()


class Place:
    pass


def kernel(cfg, qa, qg, tr, bi, bo, ei, eo, out, *scratch):
    rows, cols, counts = cfg["rows"], cfg["cols"], cfg["counts"]
    num_grad, num_act = counts
    width, act_width = cfg["width"], cfg["act_width"]
    queries, trains = qa.shape[0], tr.shape[0]
    depth_in, in_cols = bi.shape
    depth_out, out_cols = bo.shape
    piece_q, piece_t = queries // rows, trains // rows
    half_q, half_t = queries // 2, trains // 2
    it = iter(scratch)
    take = lambda n: [next(it) for _ in range(n)]
    grad_bufs, inner_bufs = take(7), take(7)
    (qa_v, qg_v, tr_v, bi_v, bo_v, ei_b, eo_q, scaled_v,
     act_part, act_own, act_out, act_in, act_full, act_t,
     pred, pred_out, pred_in) = take(17)
    grad_sems, inner_sems = take(9), take(9)
    (load_s, bi_s, bo_s, act_os, act_or, gat_s, gat_r, pred_s, pred_r) = take(9)

    me = lax.axis_index("row")
    col = lax.axis_index("col")
    place = Place()
    place.reach = cols // 4
    chips = cols // 2
    place.core = col % 2
    chip = col // 2
    low = chip < place.reach
    place.depth = jnp.where(low, chip, chips - 1 - chip)
    place.middle = place.depth == place.reach - 1
    toward = jnp.where(low, 1, -1)
    place.inward = (chip + toward) * 2 + place.core
    place.outward = (chip - toward) * 2 + place.core
    place.partner = col + 1 - 2 * place.core
    core = place.core

    def peer(step):
        return (me + step) % rows

    grad = Line(place, num_grad, half_q, cfg["wire"], grad_bufs, grad_sems, None)
    inner = Line(place, num_grad, half_t, cfg["wire"], inner_bufs, inner_sems, cfg["factor"])

    def local(src, dst, sem):
        return pltpu.make_async_copy(src, dst, sem)

    loads_qg = [local(qg.at[pl.ds(h * half_q, half_q), :], qg_v.at[h], load_s.at[h]) for h in range(2)]
    loads_tr = [local(tr.at[pl.ds(h * half_t, half_t), :], tr_v.at[h], load_s.at[2 + h]) for h in range(2)]
    load_qa = local(qa, qa_v, load_s.at[4])

    def bo_load(k):
        return local(bo.at[:, pl.ds(pl.multiple_of(k * width, width), width)], bo_v.at[k % 2], bo_s.at[k % 2])

    def bi_load(m):
        return local(bi.at[:, pl.ds(pl.multiple_of(m * act_width, act_width), act_width)],
                     bi_v.at[m % 2], bi_s.at[m % 2])

    for load in loads_qg:
        load.start()
    bo_load(0).start()
    load_qa.start()
    bi_load(0).start()
    for load in loads_tr:
        load.start()

    barrier = pltpu.get_barrier_semaphore()
    pl.semaphore_signal(barrier, inc=1, device_id={"col": place.partner}, device_id_type=MESH)
    pl.semaphore_signal(barrier, inc=1, device_id={"col": place.inward}, device_id_type=MESH)
    if place.reach > 1:
        @pl.when(place.depth > 0)
        def _():
            pl.semaphore_signal(barrier, inc=1, device_id={"col": place.outward}, device_id_type=MESH)
    for step in range(1, rows):
        pl.semaphore_signal(barrier, inc=1, device_id={"row": peer(step)}, device_id_type=MESH)
    pl.semaphore_wait(barrier, 2 + jnp.where(place.depth > 0, 1, 0) + rows - 1)

    lane = ei_b.shape[1]
    damp = damping_share * jnp.mean(ei[...]) * jnp.mean(eo[...]) * queries
    for b in range(in_cols // lane):
        at = pl.multiple_of(col * in_cols + b * lane, lane)
        ei_b[b * lane:(b + 1) * lane, :] = jnp.broadcast_to(ei[:, pl.ds(at, lane)], (lane, lane)).T
    eo_q[...] = eo[:, pl.ds(pl.multiple_of(me * out_cols, lane), out_cols)] * float(queries)
    for load in loads_qg:
        load.wait()

    def grad_step(k):
        bo_load(k).wait()

        @pl.when(k + 1 < num_grad)
        def _():
            bo_load(k + 1).start()
        basis = bo_v.at[k % 2]
        term = lambda h: jnp.dot(qg_v[h], basis[...], preferred_element_type=f32)
        grad.start(k, lambda: term(1 - core), lambda: term(core))

    def act_copy(m, step):
        return remote(act_out.at[m % 2, peer(step)], act_in.at[m, step - 1], act_os.at[m % 2, step - 1],
                      act_or.at[m, step - 1], {"row": peer(step)})

    def gather_copy(m, step):
        return remote(act_full.at[m, me], act_full.at[m, me], gat_s.at[m, step - 1],
                      gat_r.at[m, step - 1], {"row": peer(step)})

    def act_step(m):
        @pl.when(m == 0)
        def _():
            load_qa.wait()
        bi_load(m).wait()

        @pl.when(m + 1 < num_act)
        def _():
            bi_load(m + 1).start()

        @pl.when(m >= 2)
        def _():
            for step in range(1, rows):
                act_copy(m - 2, step).wait_send()
        part = jnp.dot(qa_v[...], bi_v[m % 2], preferred_element_type=f32).reshape(rows, piece_q, act_width)
        act_part[...] = part
        act_out[m % 2] = part.astype(bf16)
        for step in range(1, rows):
            act_copy(m, step).start()
        act_own[m % stash_slots] = act_part[me]

    def act_sum(m):
        total = act_own[m % stash_slots]
        for step in range(1, rows):
            act_copy(m, step).wait_recv()
            total = total + act_in[m, step - 1].astype(f32)
        act_full[m, me] = total.astype(bf16)
        for step in range(1, rows):
            gather_copy(m, step).start()

    def act_turn(m):
        for step in range(1, rows):
            gather_copy(m, step).wait_recv()
        whole = act_full[m].reshape(queries, act_width)
        act_t[pl.ds(pl.multiple_of(m * act_width, act_width), act_width), :] = whole.T
        for step in range(1, rows):
            gather_copy(m, step).wait_send()

    block = cfg["block"]

    def outer_step(k):
        @pl.when(k == 0)
        def _():
            for load in loads_tr:
                load.wait()
        grad.ready(k)
        g = grad.full[k].reshape(queries, width)
        scale_out = eo_q[:, pl.ds(pl.multiple_of(k * width, width), width)]
        for b in range(in_cols // block):
            rows_b = slice(b * block, (b + 1) * block)
            outer = jnp.dot(act_t[rows_b, :], g, preferred_element_type=f32)
            scale_in = ei_b[rows_b, :]
            scale_in = jnp.concatenate([scale_in] * (width // lane), axis=1)
            scaled_v[rows_b, :] = (outer / (scale_in * scale_out + damp)).astype(bf16)
        term = lambda h: jnp.dot(tr_v[h], scaled_v[...], preferred_element_type=f32)
        inner.start(k, lambda: term(1 - core), lambda: term(core))

    def pred_step(k):
        inner.ready(k)
        bo_load(k).wait()

        @pl.when(k + 1 < num_grad)
        def _():
            bo_load(k + 1).start()
        part = inner.full[k].reshape(trains, width)
        term = lax.dot_general(part, bo_v[k % 2], (((1,), (1,)), ((), ())), preferred_element_type=f32)

        @pl.when(k == 0)
        def _():
            pred[...] = term

        @pl.when(k > 0)
        def _():
            pred[...] += term

    lead = max(act_every * (num_act - 1) + gather_lag, num_grad)
    steps = lead + num_grad + 7

    def at(s, lag, count, fn):
        k = s - lag

        @pl.when(jnp.logical_and(k >= 0, k < count))
        def _():
            fn(k)

    def at_every(s, lag, count, fn):
        k = s - lag
        m = k // act_every

        @pl.when(jnp.logical_and(jnp.logical_and(k >= 0, m < count), k % act_every == 0))
        def _():
            fn(m)

    def timestep(s, carry):
        at(s, 0, num_grad, grad_step)
        at_every(s, 0, num_act, act_step)
        at(s, 0, num_grad, grad.pair_sum)
        at(s, 1, num_grad, grad.add_inward)
        at(s, 2, num_grad, grad.add_across)
        at_every(s, 2, num_act, act_sum)
        at(s, 4, num_grad, grad.relay)
        at_every(s, gather_lag, num_act, act_turn)
        at(s, lead + 1, num_grad, inner.pair_sum)
        at(s, lead, num_grad, outer_step)
        at(s, lead + 2, num_grad, inner.add_inward)
        at(s, lead + 3, num_grad, inner.add_across)
        at(s, lead + 5, num_grad, inner.relay)

        @pl.when(s == lead)
        def _():
            bo_load(0).start()
        at(s, lead + 6, num_grad, pred_step)
        return carry

    lax.fori_loop(0, steps, timestep, 0)

    def pred_copy(step):
        return remote(pred_out.at[peer(step)], pred_in.at[step - 1], pred_s.at[step - 1],
                      pred_r.at[step - 1], {"row": peer(step)})

    pred_out[...] = pred[...].astype(bf16).reshape(pred_out.shape)
    for step in range(1, rows):
        pred_copy(step).start()
    total = pred[pl.ds(pl.multiple_of(me * piece_t, 8), piece_t), :]
    for step in range(1, rows):
        pred_copy(step).wait_recv()
        total = total + pred_in[step - 1].astype(f32)
    out[...] = total

    grad.drain()
    inner.drain()
    for m in range(max(0, num_act - 2), num_act):
        for step in range(1, rows):
            act_copy(m, step).wait_send()
    for step in range(1, rows):
        pred_copy(step).wait_send()


def per_device(mesh_shape, query_act, query_grad, train_rot, basis_in, basis_out, eig_in, eig_out):
    rows, cols = mesh_shape["row"], mesh_shape["col"]
    queries, depth_in = query_act.shape
    trains = train_rot.shape[0]
    in_cols = basis_in.shape[1]
    depth_out, out_cols = basis_out.shape
    width = min(chunk_width, out_cols)
    act_width = min(chunk_width, in_cols)
    num_grad, num_act = out_cols // width, in_cols // act_width
    wire = bf16 if cols // 4 <= 2 else f32
    cfg = dict(rows=rows, cols=cols, counts=(num_grad, num_act), width=width, act_width=act_width, wire=wire,
               factor=1.0 / float(eig_in.shape[0]) ** 0.5, block=min(512, in_cols))
    dma = pltpu.SemaphoreType.DMA
    half_q, half_t = queries // 2, trains // 2
    piece_q, piece_t = queries // rows, trains // rows
    scratch = (
        Line.buffers(num_grad, half_q, width, wire)
        + Line.buffers(num_grad, half_t, width, wire)
        + [
            pltpu.VMEM((queries, depth_in), bf16),
            pltpu.VMEM((2, half_q, depth_out), bf16),
            pltpu.VMEM((2, half_t, in_cols), bf16),
            pltpu.VMEM((2, depth_in, act_width), bf16),
            pltpu.VMEM((2, depth_out, width), bf16),
            pltpu.VMEM((in_cols, 128), f32),
            pltpu.VMEM((1, out_cols), f32),
            pltpu.VMEM((in_cols, width), bf16),
            pltpu.VMEM((rows, piece_q, act_width), f32),
            pltpu.VMEM((stash_slots, piece_q, act_width), f32),
            pltpu.VMEM((2, rows, piece_q, act_width), bf16),
            pltpu.VMEM((num_act, rows - 1, piece_q, act_width), bf16),
            pltpu.VMEM((num_act, rows, piece_q, act_width), bf16),
            pltpu.VMEM((in_cols, queries), bf16),
            pltpu.VMEM((trains, depth_out), f32),
            pltpu.VMEM((rows, piece_t, depth_out), bf16),
            pltpu.VMEM((rows - 1, piece_t, depth_out), bf16),
        ]
        + Line.semaphores(num_grad) + Line.semaphores(num_grad)
        + [dma((5,)), dma((2,)), dma((2,)), dma((2, rows - 1)), dma((num_act, rows - 1)),
           dma((num_act, rows - 1)), dma((num_act, rows - 1)), dma((rows - 1,)), dma((rows - 1,))]
    )
    hbm = pl.BlockSpec(memory_space=pl.ANY)
    vmem = pl.BlockSpec(memory_space=pltpu.VMEM)
    return pl.pallas_call(
        functools.partial(kernel, cfg),
        out_shape=jax.ShapeDtypeStruct((piece_t, depth_out), f32),
        in_specs=[hbm] * 5 + [vmem] * 2,
        out_specs=vmem,
        scratch_shapes=scratch,
        compiler_params=pltpu.CompilerParams(
            collective_id=0, has_side_effects=True, vmem_limit_bytes=67043328
        ),
    )(query_act, query_grad, train_rot, basis_in, basis_out,
      eig_in.reshape(1, -1), eig_out.reshape(1, -1))


def solution(mesh):
    in_specs = (
        P(None, "row"),
        P(None, "col"),
        P(None, "col"),
        P("row", "col"),
        P("col", "row"),
        P(),
        P(),
    )
    return jax.shard_map(
        functools.partial(per_device, dict(mesh.shape)), mesh=mesh, in_specs=in_specs,
        out_specs=P("row", "col"), check_vma=False,
    )
```

profile of v0, /device:TPU:0, one launch (start us, length us, event | category | flops | bytes accessed | tf_op | source)
XLA Modules:
  0.0 189.4 jit_solution(58675056727574748)
XLA Ops:
  0.0 187.3 %shard_map.73 = f32[96,2048]{1,0:T(8,128)} custom-call(bf16[768,4096]{1,0:T(8,128)(2,1)} %qa.1, bf16[768,2048]{1,0:T(8,128)(2,1)} %qg.1, bf16[384,2048]{1,0:T(8,128)(2,1)} %tr.1, bf16[4096,2048]{1,0:T(8,128)(2,1)} %bi.1, bf16[2048,4096]{1,0:T(8,128)(2,1)} %bo.1, f32[1,16384]{1,0:T(1,128)} %bitcast.2, f32[1,16384]{1,0:T(1,128)} %bitcast.3), custom_call_target="tpu_custom_call" | custom-call | tf_op jit(solution)/shard_map/pallas_call | solution.py:446
  187.3 2.1 %copy.9 = f32[96,2048]{1,0:T(8,128)} copy(f32[96,2048]{1,0:T(8,128)} %shard_map.73) | data formatting | bytes 1572864
where the time goes:
time: 190 us; the launch traced here: 189 us
  Pallas kernels  187 us (98%)
  local copies, waits for them, and re-layouts  2.06 us (1%)
    pallas_call x1, Pallas kernels, per_device(): pl.pallas_call(functools.partial(kernel, cfg), out_shape=jax.ShapeDtypeSt...  187 us

commit v1 on v0

v1 whole, which is shorter than its diff:
```python
import functools
import math

import jax
import jax.numpy as jnp
from jax import lax
from jax.experimental import pallas as pl
from jax.experimental.pallas import tpu as pltpu
from jax.sharding import PartitionSpec as P

damping_share = 0.1
chunk_width = 256
send_slots = 3
act_slots = 4
grad_slots = 4
grad_held = 6
inner_held = 7
inner_pairs = 4
inner_pair_lag = 2
inner_passes = 2
grad_lags = (1, 3, 5)
act_lags = (2, 4, 6, 8)
act_pace = (1, 1)
inner_reps = 2
inner_lags = (4, 6, 8, 9)
MESH = pl.DeviceIdType.MESH
f32 = jnp.float32
bf16 = jnp.bfloat16


def remote(src, dst, send, recv, device):
    return pltpu.make_async_remote_copy(
        src_ref=src, dst_ref=dst, send_sem=send, recv_sem=recv,
        device_id=device, device_id_type=MESH,
    )


class Line:
    def __init__(self, place, count, slots, held, pairs, passes, half, wire, bufs, sems, scale):
        self.place, self.count, self.half, self.wire, self.scale = place, count, half, wire, scale
        self.slots, self.held, self.pairs, self.passes = slots, held, pairs, passes
        (self.pair_out, self.pair_in, self.stash, self.out, self.inward_in, self.across_in, self.full, self.theirs) = bufs
        (self.pair_s, self.pair_r, self.out_s, self.inward_r, self.across_r,
         self.back_s, self.back_r, self.mate_s, self.mate_r) = sems

    @staticmethod
    def buffers(count, slots, held, pairs, passes, half, width, wire):
        return [
            pltpu.VMEM((pairs, half, width), f32),
            pltpu.VMEM((pairs, half, width), f32),
            pltpu.VMEM((slots, half, width), f32),
            pltpu.VMEM((send_slots, half, width), wire),
            pltpu.VMEM((held, half, width), wire),
            pltpu.VMEM((held, half, width), wire),
            pltpu.VMEM((count, 2, half, width), bf16),
            pltpu.VMEM((count, half, width) if passes > 1 else (8, 128), f32),
        ]

    @staticmethod
    def semaphores(count, pairs):
        dma = pltpu.SemaphoreType.DMA
        return [dma((pairs,)), dma((count,)), dma((send_slots,)), dma((count,)), dma((count,)),
                dma((count,)), dma((count,)), dma((count,)), dma((count,))]

    def pair(self, k):
        slot = k % self.pairs
        return remote(self.pair_out.at[slot], self.pair_in.at[slot], self.pair_s.at[slot],
                      self.pair_r.at[k], {"col": self.place.partner})

    def inward(self, k):
        slot = k % send_slots
        return remote(self.out.at[slot], self.inward_in.at[k % self.held], self.out_s.at[slot],
                      self.inward_r.at[k], {"col": self.place.inward})

    def across(self, k):
        slot = k % send_slots
        return remote(self.out.at[slot], self.across_in.at[k % self.held], self.out_s.at[slot],
                      self.across_r.at[k], {"col": self.place.inward})

    def back(self, k):
        piece = self.full.at[k, self.place.core]
        return remote(piece, piece, self.back_s.at[k], self.back_r.at[k], {"col": self.place.outward})

    def mate(self, k):
        piece = self.full.at[k, self.place.core]
        return remote(piece, piece, self.mate_s.at[k], self.mate_r.at[k], {"col": self.place.partner})

    def start(self, k, theirs, mine, turn=0):
        slot = k % self.slots

        def add(ref, at, value):
            if turn == 0:
                ref[at] = value
            else:
                ref[at] += value
        if turn < self.passes - 1:
            add(self.theirs, k, theirs())
            add(self.stash, slot, mine())
            return

        @pl.when(k >= self.pairs)
        def _():
            self.pair(k - self.pairs).wait_send()
        term = theirs()
        self.pair_out[k % self.pairs] = term if turn == 0 else term + self.theirs[k]
        self.pair(k).start()
        add(self.stash, slot, mine())

    def send_out(self, k, total, first):
        @pl.when(k >= send_slots)
        def _():
            self.inward(k - send_slots).wait_send()
        self.out[k % send_slots] = total.astype(self.wire)
        if self.place.reach == 1:
            self.across(k).start()
        elif first:
            self.inward(k).start()
        else:
            @pl.when(self.place.middle)
            def _():
                self.across(k).start()
            @pl.when(jnp.logical_not(self.place.middle))
            def _():
                self.inward(k).start()

    def pair_sum(self, k):
        self.pair(k).wait_recv()
        slot = k % self.slots
        total = self.stash[slot] + self.pair_in[k % self.pairs]
        self.stash[slot] = total

        @pl.when(self.place.depth == 0)
        def _():
            self.send_out(k, total, True)

    def add_inward(self, k):
        if self.place.reach == 1:
            return

        @pl.when(self.place.depth > 0)
        def _():
            self.inward(k).wait_recv()
            slot = k % self.slots
            total = self.stash[slot] + self.inward_in[k % self.held].astype(f32)
            self.stash[slot] = total
            self.send_out(k, total, False)

    def add_across(self, k):
        @pl.when(self.place.middle)
        def _():
            self.across(k).wait_recv()
            total = self.stash[k % self.slots] + self.across_in[k % self.held].astype(f32)
            if self.scale is not None:
                total = total * self.scale
            self.full[k, self.place.core] = total.astype(bf16)
            if self.place.reach > 1:
                self.back(k).start()
            self.mate(k).start()

    def relay(self, k):
        if self.place.reach == 1:
            return

        @pl.when(jnp.logical_not(self.place.middle))
        def _():
            self.back(k).wait_recv()

            @pl.when(self.place.depth > 0)
            def _():
                self.back(k).start()
            self.mate(k).start()

    def ready(self, k):
        self.mate(k).wait_recv()
        self.mate(k).wait_send()
        if self.place.reach > 1:
            @pl.when(self.place.depth > 0)
            def _():
                self.back(k).wait_send()

    def drain(self):
        for k in range(max(0, self.count - self.pairs), self.count):
            self.pair(k).wait_send()
        for k in range(max(0, self.count - send_slots), self.count):
            self.inward(k).wait_send()


class Place:
    pass


def kernel(cfg, qa, qg, tr, bi, bo, ei, eo, out, *scratch):
    rows, cols, counts = cfg["rows"], cfg["cols"], cfg["counts"]
    num_grad, num_act = counts
    width, act_width = cfg["width"], cfg["act_width"]
    queries, trains = qa.shape[0], tr.shape[0]
    depth_in, in_cols = bi.shape
    depth_out, out_cols = bo.shape
    piece_q, piece_t = queries // rows, trains // rows
    half_q, half_t = queries // 2, trains // 2
    it = iter(scratch)
    take = lambda n: [next(it) for _ in range(n)]
    grad_bufs, inner_bufs = take(8), take(8)
    (qa_v, qg_v, tr_v, wide_v, bo_v, ei_b, eo_q, scaled_v,
     act_part, act_own, act_out, act_out2, act_in, act_in2, act_full, act_t,
     pred, pred_out, pred_in, damp_s) = take(20)
    grad_sems, inner_sems = take(9), take(9)
    (load_s, bi_s, bo_s, group_s, act_os, act_or, act_os2, act_or2, gat_s, gat_r, gat_s2, gat_r2,
     pred_s, pred_r) = take(14)

    me = lax.axis_index("row")
    col = lax.axis_index("col")
    place = Place()
    place.reach = cols // 4
    chips = cols // 2
    place.core = col % 2
    chip = col // 2
    low = chip < place.reach
    place.depth = jnp.where(low, chip, chips - 1 - chip)
    place.middle = place.depth == place.reach - 1
    toward = jnp.where(low, 1, -1)
    place.inward = (chip + toward) * 2 + place.core
    place.outward = (chip - toward) * 2 + place.core
    place.partner = col + 1 - 2 * place.core
    core = place.core

    def peer(step):
        return (me + step) % rows

    grad = Line(place, num_grad, grad_slots, cfg["held"], 2, 1, half_q, cfg["wire"], grad_bufs, grad_sems, None)
    inner = Line(place, num_grad, num_grad, cfg["inner_held"], inner_pairs, cfg["passes"], half_t, cfg["wire"], inner_bufs, inner_sems, cfg["factor"])

    def local(src, dst, sem):
        return pltpu.make_async_copy(src, dst, sem)

    loads_qg = [local(qg.at[pl.ds(h * half_q, half_q), :], qg_v.at[h], load_s.at[h]) for h in range(2)]
    loads_tr = [local(tr.at[pl.ds(h * half_t, half_t), :], tr_v.at[h], load_s.at[2 + h]) for h in range(2)]
    load_qa = local(qa, qa_v, load_s.at[4])

    ratio = depth_in // depth_out
    group = cfg["group"]

    def bo_load(k):
        return local(bo.at[:, pl.ds(pl.multiple_of(k * width, width), width)], bo_v.at[k % 2], bo_s.at[k % 2])

    def bi_load(m):
        from_cols = pl.ds(pl.multiple_of(m * act_width, act_width), act_width)
        return [local(bi.at[pl.ds(h * depth_out, depth_out), from_cols],
                      wide_v.at[:, pl.ds(pl.multiple_of((m % 2 * ratio + h) * act_width, act_width), act_width)],
                      bi_s.at[m % 2, h]) for h in range(ratio)]

    def group_load(g):
        span = group * width
        return local(bo.at[:, pl.ds(pl.multiple_of(g * span, span), span)], wide_v, group_s)

    for load in loads_qg:
        load.start()
    bo_load(0).start()
    load_qa.start()
    for load in bi_load(0):
        load.start()
    for load in loads_tr:
        load.start()

    barrier = pltpu.get_barrier_semaphore()
    pl.semaphore_signal(barrier, inc=1, device_id={"col": place.partner}, device_id_type=MESH)
    pl.semaphore_signal(barrier, inc=1, device_id={"col": place.inward}, device_id_type=MESH)
    if place.reach > 1:
        @pl.when(place.depth > 0)
        def _():
            pl.semaphore_signal(barrier, inc=1, device_id={"col": place.outward}, device_id_type=MESH)
    for step in range(1, rows):
        pl.semaphore_signal(barrier, inc=1, device_id={"row": peer(step)}, device_id_type=MESH)
    pl.semaphore_wait(barrier, 2 + jnp.where(place.depth > 0, 1, 0) + rows - 1)

    lane = ei_b.shape[1]

    def eigen_step():
        damp_s[0] = damping_share * jnp.mean(ei[...]) * jnp.mean(eo[...]) * queries
        for b in range(in_cols // lane):
            at = pl.multiple_of(col * in_cols + b * lane, lane)
            ei_b[b * lane:(b + 1) * lane, :] = jnp.broadcast_to(ei[:, pl.ds(at, lane)], (lane, lane)).T
        eo_q[...] = eo[:, pl.ds(pl.multiple_of(me * out_cols, lane), out_cols)] * float(queries)

    for load in loads_qg:
        load.wait()

    def grad_step(k):
        bo_load(k).wait()

        @pl.when(k + 1 < num_grad)
        def _():
            bo_load(k + 1).start()
        basis = bo_v.at[k % 2]
        term = lambda h: jnp.dot(qg_v[h], basis[...], preferred_element_type=f32)
        grad.start(k, lambda: term(1 - core), lambda: term(core))

    first, second = cfg["split"]

    def axes(m):
        if first != second:
            return me % first, me // first, lambda u, v: v * first + u
        flip = m % 2
        high, low = me // first, me % first
        return (jnp.where(flip == 0, low, high), jnp.where(flip == 0, high, low),
                lambda u, v: jnp.where(flip == 0, v * first + u, u * first + v))

    def first_copy(m, step):
        u, v, row = axes(m)
        to = (u + step) % first
        return remote(act_out.at[m % 2, to], act_in.at[m, step - 1], act_os.at[m % 2, step - 1],
                      act_or.at[m, step - 1], {"row": row(to, v)})

    def second_copy(m, step):
        u, v, row = axes(m)
        to = (v + step) % second
        return remote(act_out2.at[m % 2, to], act_in2.at[m, step - 1], act_os2.at[m % 2, step - 1],
                      act_or2.at[m, step - 1], {"row": row(u, to)})

    def second_gather(m, step):
        u, v, row = axes(m)
        piece = act_full.at[m, me]
        return remote(piece, piece, gat_s2.at[m, step - 1], gat_r2.at[m, step - 1],
                      {"row": row(u, (v + step) % second)})

    def first_gather(m, step, which):
        u, v, row = axes(m)
        piece = act_full.at[m, row(u, which)]
        return remote(piece, piece, gat_s.at[m, step - 1, which], gat_r.at[m, step - 1, which],
                      {"row": row((u + step) % first, v)})

    def act_step(m):
        @pl.when(m == 0)
        def _():
            load_qa.wait()
        for load in bi_load(m):
            load.wait()

        @pl.when(m + 1 < num_act)
        def _():
            for load in bi_load(m + 1):
                load.start()

        @pl.when(m >= 2)
        def _():
            for step in range(1, first):
                first_copy(m - 2, step).wait_send()
        part = None
        for h in range(ratio):
            basis = wide_v[:, pl.ds(pl.multiple_of((m % 2 * ratio + h) * act_width, act_width), act_width)]
            term = jnp.dot(qa_v[:, h * depth_out:(h + 1) * depth_out], basis, preferred_element_type=f32)
            part = term if part is None else part + term
        act_part[...] = part.reshape(rows, piece_q, act_width)
        u, v, row = axes(m)
        for i in range(first):
            for j in range(second):
                act_out[m % 2, i, j] = act_part[row(i, j)].astype(bf16)
        for step in range(1, first):
            first_copy(m, step).start()
        for j in range(second):
            act_own[m % act_slots, j] = act_part[row(u, j)]

    def act_first_sum(m):
        @pl.when(m >= 2)
        def _():
            for step in range(1, second):
                second_copy(m - 2, step).wait_send()
        for step in range(1, first):
            first_copy(m, step).wait_recv()
        for j in range(second):
            total = act_own[m % act_slots, j]
            for step in range(1, first):
                total = total + act_in[m, step - 1, j].astype(f32)
            act_own[m % act_slots, j] = total
            act_out2[m % 2, j] = total.astype(bf16)
        for step in range(1, second):
            second_copy(m, step).start()

    def act_second_sum(m):
        u, v, row = axes(m)
        total = act_own[m % act_slots, v]
        for step in range(1, second):
            second_copy(m, step).wait_recv()
            total = total + act_in2[m, step - 1].astype(f32)
        act_full[m, me] = total.astype(bf16)
        for step in range(1, second):
            second_gather(m, step).start()

    def act_relay(m):
        for step in range(1, second):
            second_gather(m, step).wait_recv()
        for step in range(1, first):
            for j in range(second):
                first_gather(m, step, j).start()

    def act_turn(m):
        for step in range(1, first):
            for j in range(second):
                first_gather(m, step, j).wait_recv()
        whole = act_full[m].reshape(queries, act_width)
        act_t[pl.ds(pl.multiple_of(m * act_width, act_width), act_width), :] = whole.T
        for step in range(1, second):
            second_gather(m, step).wait_send()
        for step in range(1, first):
            for j in range(second):
                first_gather(m, step, j).wait_send()

    block = cfg["block"]

    passes = cfg["passes"]
    span = in_cols // passes

    def outer_step(turn, k):
        if turn == 0:
            @pl.when(k == 0)
            def _():
                for load in loads_tr:
                    load.wait()
            grad.ready(k)
        damp = damp_s[0]
        g = grad.full[k].reshape(queries, width)
        scale_out = eo_q[:, pl.ds(pl.multiple_of(k * width, width), width)]
        for b in range(span // block):
            here = slice(turn * span + b * block, turn * span + (b + 1) * block)
            outer = jnp.dot(act_t[here, :], g, preferred_element_type=f32)
            scale_in = jnp.concatenate([ei_b[here, :]] * (width // lane), axis=1)
            scaled_v[b * block:(b + 1) * block, :] = (outer / (scale_in * scale_out + damp)).astype(bf16)
        part = slice(turn * span, (turn + 1) * span)
        term = lambda h: jnp.dot(tr_v[h, :, part], scaled_v[...], preferred_element_type=f32)
        inner.start(k, lambda: term(1 - core), lambda: term(core), turn)

    def pred_step(k):
        inner.ready(k)

        @pl.when(k % group == group - 1)
        def _():
            g = k // group
            group_load(g).wait()
            part = jnp.concatenate(
                [inner.full[g * group + j].reshape(trains, width) for j in range(group)], axis=1)
            term = lax.dot_general(part, wide_v[...], (((1,), (1,)), ((), ())), preferred_element_type=f32)

            @pl.when(g == 0)
            def _():
                pred[...] = term

            @pl.when(g > 0)
            def _():
                pred[...] += term

            @pl.when(k + 1 < num_grad)
            def _():
                group_load(g + 1).start()

    def turned(m):
        return act_pace[1] * (m // act_pace[0]) + m % act_pace[0] + act_lags[3]

    after = grad_lags[2] + 1
    relayed = max(k + after - k // inner_reps for k in range(num_grad))
    starts = [turned((turn + 1) * num_act // passes - 1) for turn in range(passes)]
    start = starts[-1] = max(starts[-1], relayed, num_grad - 1)
    steps = max(start + -(-(num_grad + inner_lags[3]) // inner_reps), num_grad + after)

    def at(s, lag, count, fn):
        k = s - lag

        @pl.when(jnp.logical_and(k >= 0, k < count))
        def _():
            fn(k)

    def paced(s, lag, fn):
        k = s - lag
        chunks, period = act_pace
        m = chunks * (k // period) + k % period

        @pl.when(jnp.logical_and(jnp.logical_and(k >= 0, k % period < chunks), m < num_act))
        def _():
            fn(m)

    def early_pass(turn, s):
        def one(r, carry):
            fast = r < inner_reps
            k = jnp.where(fast, (s - starts[turn]) * inner_reps + r, s - after)
            due = jnp.where(fast, k + after <= s, starts[turn] + k // inner_reps < s)

            @pl.when(jnp.logical_and(due, jnp.logical_and(k >= 0, k < num_grad)))
            def _():
                outer_step(turn, k)
            return carry
        lax.fori_loop(0, inner_reps + 1, one, 0)

    def last_step(u):
        at(u, inner_pair_lag, num_grad, inner.pair_sum)
        at(u, 0, num_grad, lambda k: outer_step(passes - 1, k))
        at(u, inner_lags[0], num_grad, inner.add_inward)
        at(u, inner_lags[1], num_grad, inner.add_across)
        at(u, inner_lags[2], num_grad, inner.relay)
        at(u, inner_lags[3], num_grad, pred_step)

    def inner_steps(s):
        for turn in range(passes - 1):
            @pl.when(s >= starts[turn])
            def _():
                early_pass(turn, s)

        @pl.when(s >= start)
        def _():
            first_u = (s - start) * inner_reps
            lax.fori_loop(0, inner_reps, lambda r, c: (last_step(first_u + r), c)[1], 0)

    def timestep(s, carry):
        at(s, 0, num_grad, grad_step)
        paced(s, act_lags[1], act_second_sum)
        paced(s, 0, act_step)
        at(s, 0, num_grad, grad.pair_sum)
        at(s, grad_lags[0], num_grad, grad.add_inward)
        at(s, grad_lags[1], num_grad, grad.add_across)
        paced(s, act_lags[0], act_first_sum)
        paced(s, act_lags[2], act_relay)
        at(s, grad_lags[2], num_grad, grad.relay)
        paced(s, act_lags[3], act_turn)

        @pl.when(s == 1)
        def _():
            eigen_step()

        @pl.when(s == start)
        def _():
            group_load(0).start()

        inner_steps(s)
        return carry

    lax.fori_loop(0, steps, timestep, 0)

    def pred_copy(step):
        return remote(pred_out.at[step - 1], pred_in.at[step - 1], pred_s.at[step - 1],
                      pred_r.at[step - 1], {"row": peer(step)})

    def pred_piece(step):
        return pred[pl.ds(pl.multiple_of(peer(step) * piece_t, 8), piece_t), :]

    for step in range(1, rows):
        pred_out[step - 1] = pred_piece(step).astype(bf16)
        pred_copy(step).start()
    total = pred_piece(0)
    for step in range(1, rows):
        pred_copy(step).wait_recv()
        total = total + pred_in[step - 1].astype(f32)
    out[...] = total

    grad.drain()
    inner.drain()
    for m in range(max(0, num_act - 2), num_act):
        for step in range(1, first):
            first_copy(m, step).wait_send()
        for step in range(1, second):
            second_copy(m, step).wait_send()
    for step in range(1, rows):
        pred_copy(step).wait_send()


def per_device(mesh_shape, query_act, query_grad, train_rot, basis_in, basis_out, eig_in, eig_out):
    rows, cols = mesh_shape["row"], mesh_shape["col"]
    queries, depth_in = query_act.shape
    trains = train_rot.shape[0]
    in_cols = basis_in.shape[1]
    depth_out, out_cols = basis_out.shape
    width = min(chunk_width, out_cols)
    act_width = min(chunk_width, in_cols)
    num_grad, num_act = out_cols // width, in_cols // act_width
    wire = bf16 if cols // 4 <= 2 else f32
    side = math.isqrt(rows)
    first, second = (side, side) if side * side == rows else (rows, 1)
    held = min(grad_held, num_grad)
    passes = inner_passes if num_act % inner_passes == 0 else 1
    group = 2 * (depth_in // depth_out)
    cfg = dict(group=group, passes=passes, inner_held=min(inner_held, num_grad), split=(first, second), held=held, rows=rows, cols=cols, counts=(num_grad, num_act), width=width, act_width=act_width, wire=wire,
               factor=1.0 / float(eig_in.shape[0]) ** 0.5, block=min(512, in_cols // passes))
    dma = pltpu.SemaphoreType.DMA
    half_q, half_t = queries // 2, trains // 2
    piece_q, piece_t = queries // rows, trains // rows
    scratch = (
        Line.buffers(num_grad, grad_slots, held, 2, 1, half_q, width, wire)
        + Line.buffers(num_grad, num_grad, min(inner_held, num_grad), inner_pairs, passes, half_t, width, wire)
        + [
            pltpu.VMEM((queries, depth_in), bf16),
            pltpu.VMEM((2, half_q, depth_out), bf16),
            pltpu.VMEM((2, half_t, in_cols), bf16),
            pltpu.VMEM((depth_out, group * width), bf16),
            pltpu.VMEM((2, depth_out, width), bf16),
            pltpu.VMEM((in_cols, 128), f32),
            pltpu.VMEM((1, out_cols), f32),
            pltpu.VMEM((in_cols // passes, width), bf16),
            pltpu.VMEM((rows, piece_q, act_width), f32),
            pltpu.VMEM((act_slots, second, piece_q, act_width), f32),
            pltpu.VMEM((2, first, second, piece_q, act_width), bf16),
            pltpu.VMEM((2, second, piece_q, act_width), bf16),
            pltpu.VMEM((num_act, first - 1, second, piece_q, act_width), bf16),
            pltpu.VMEM((num_act, max(second - 1, 1), piece_q, act_width), bf16),
            pltpu.VMEM((num_act, rows, piece_q, act_width), bf16),
            pltpu.VMEM((in_cols, queries), bf16),
            pltpu.VMEM((trains, depth_out), f32),
            pltpu.VMEM((rows - 1, piece_t, depth_out), bf16),
            pltpu.VMEM((rows - 1, piece_t, depth_out), bf16),
            pltpu.SMEM((1,), f32),
        ]
        + Line.semaphores(num_grad, 2) + Line.semaphores(num_grad, inner_pairs)
        + [dma((5,)), dma((2, depth_in // depth_out)), dma((2,)), dma(()), dma((2, first - 1)), dma((num_act, first - 1)),
           dma((2, max(second - 1, 1))), dma((num_act, max(second - 1, 1))),
           dma((num_act, first - 1, second)), dma((num_act, first - 1, second)),
           dma((num_act, max(second - 1, 1))), dma((num_act, max(second - 1, 1))),
           dma((rows - 1,)), dma((rows - 1,))]
    )
    hbm = pl.BlockSpec(memory_space=pl.ANY)
    vmem = pl.BlockSpec(memory_space=pltpu.VMEM)
    return pl.pallas_call(
        functools.partial(kernel, cfg),
        out_shape=jax.ShapeDtypeStruct((piece_t, depth_out), f32),
        in_specs=[hbm] * 5 + [vmem] * 2,
        out_specs=vmem,
        scratch_shapes=scratch,
        compiler_params=pltpu.CompilerParams(
            collective_id=0, has_side_effects=True, vmem_limit_bytes=67043328
        ),
    )(query_act, query_grad, train_rot, basis_in, basis_out,
      eig_in.reshape(1, -1), eig_out.reshape(1, -1))


def solution(mesh):
    in_specs = (
        P(None, "row"),
        P(None, "col"),
        P(None, "col"),
        P("row", "col"),
        P("col", "row"),
        P(),
        P(),
    )
    return jax.shard_map(
        functools.partial(per_device, dict(mesh.shape)), mesh=mesh, in_specs=in_specs,
        out_specs=P("row", "col"), check_vma=False,
    )
```

time: 190 us -> 165 us (0.87)
  Pallas kernels: 187 us -> 163 us
    pallas_call x1, Pallas kernels: 187 us -> 163 us  [per_device(): pl.pallas_call(functools.partial(kernel, cfg), out_shape=jax.ShapeDtypeSt...]
where the time goes in v1:
time: 165 us
  Pallas kernels  163 us (99%)
  local copies, waits for them, and re-layouts  2.06 us (1%)
    pallas_call x1, Pallas kernels, per_device(): pl.pallas_call(functools.partial(kernel, cfg), out_shape=jax.ShapeDtypeSt...  163 us

profile of v1, /device:TPU:0, one launch (start us, length us, event | category | flops | bytes accessed | tf_op | source)
XLA Modules:
  0.0 164.8 jit_solution(8460818835923640142)
XLA Ops:
  0.0 162.8 %shard_map.73 = f32[96,2048]{1,0:T(8,128)} custom-call(bf16[768,4096]{1,0:T(8,128)(2,1)} %qa.1, bf16[768,2048]{1,0:T(8,128)(2,1)} %qg.1, bf16[384,2048]{1,0:T(8,128)(2,1)} %tr.1, bf16[4096,2048]{1,0:T(8,128)(2,1)} %bi.1, bf16[2048,4096]{1,0:T(8,128)(2,1)} %bo.1, f32[1,16384]{1,0:T(1,128)} %bitcast.2, f32[1,16384]{1,0:T(1,128)} %bitcast.3), custom_call_target="tpu_custom_call" | custom-call | tf_op jit(solution)/shard_map/pallas_call | solution.py:617
  162.8 2.1 %copy.9 = f32[96,2048]{1,0:T(8,128)} copy(f32[96,2048]{1,0:T(8,128)} %shard_map.73) | data formatting | bytes 1572864

commit v2 on v1

--- a/solution.py
+++ b/solution.py
@@ -14,7 +14,8 @@
 act_slots = 4
 grad_slots = 4
 grad_held = 6
-inner_held = 7
+inner_held = 8
+pred_parts = 4
 inner_pairs = 4
 inner_pair_lag = 2
 inner_passes = 2
@@ -22,7 +23,7 @@
 act_lags = (2, 4, 6, 8)
 act_pace = (1, 1)
 inner_reps = 2
-inner_lags = (4, 6, 8, 9)
+inner_lags = (4, 7, 9, 10)
 MESH = pl.DeviceIdType.MESH
 f32 = jnp.float32
 bf16 = jnp.bfloat16
@@ -429,16 +430,22 @@
         term = lambda h: jnp.dot(tr_v[h, :, part], scaled_v[...], preferred_element_type=f32)
         inner.start(k, lambda: term(1 - core), lambda: term(core), turn)
 
+    def pred_operand(g):
+        group_load(g).wait()
+        return jnp.concatenate([inner.full[g * group + j].reshape(trains, width) for j in range(group)], axis=1)
+
+    def pred_term(part, basis):
+        return lax.dot_general(part, basis, (((1,), (1,)), ((), ())), preferred_element_type=f32)
+
+    num_groups = num_grad // group
+
     def pred_step(k):
         inner.ready(k)
 
-        @pl.when(k % group == group - 1)
+        @pl.when(jnp.logical_and(k % group == group - 1, k + 1 < num_grad))
         def _():
             g = k // group
-            group_load(g).wait()
-            part = jnp.concatenate(
-                [inner.full[g * group + j].reshape(trains, width) for j in range(group)], axis=1)
-            term = lax.dot_general(part, wide_v[...], (((1,), (1,)), ((), ())), preferred_element_type=f32)
+            term = pred_term(pred_operand(g), wide_v[...])
 
             @pl.when(g == 0)
             def _():
@@ -447,10 +454,7 @@
             @pl.when(g > 0)
             def _():
                 pred[...] += term
-
-            @pl.when(k + 1 < num_grad)
-            def _():
-                group_load(g + 1).start()
+            group_load(g + 1).start()
 
     def turned(m):
         return act_pace[1] * (m // act_pace[0]) + m % act_pace[0] + act_lags[3]
@@ -533,21 +537,30 @@
 
     lax.fori_loop(0, steps, timestep, 0)
 
-    def pred_copy(step):
-        return remote(pred_out.at[step - 1], pred_in.at[step - 1], pred_s.at[step - 1],
-                      pred_r.at[step - 1], {"row": peer(step)})
-
-    def pred_piece(step):
-        return pred[pl.ds(pl.multiple_of(peer(step) * piece_t, 8), piece_t), :]
-
-    for step in range(1, rows):
-        pred_out[step - 1] = pred_piece(step).astype(bf16)
-        pred_copy(step).start()
-    total = pred_piece(0)
-    for step in range(1, rows):
-        pred_copy(step).wait_recv()
-        total = total + pred_in[step - 1].astype(f32)
-    out[...] = total
+    def pred_copy(step, p):
+        at_cols = slice(p * part_cols, (p + 1) * part_cols)
+        return remote(pred_out.at[step - 1, :, at_cols], pred_in.at[step - 1, :, at_cols], pred_s.at[step - 1, p],
+                      pred_r.at[step - 1, p], {"row": peer(step)})
+
+    def pred_piece(step, p):
+        return pred[pl.ds(pl.multiple_of(peer(step) * piece_t, 8), piece_t), p * part_cols:(p + 1) * part_cols]
+
+    parts = cfg["pred_parts"]
+    part_cols = depth_out // parts
+    last = pred_operand(num_groups - 1)
+    for p in range(parts):
+        here = slice(p * part_cols, (p + 1) * part_cols)
+        term = pred_term(last, wide_v[here, :])
+        pred[:, here] = term if num_groups == 1 else pred[:, here] + term
+        for step in range(1, rows):
+            pred_out[step - 1, :, here] = pred_piece(step, p).astype(bf16)
+            pred_copy(step, p).start()
+    for p in range(parts):
+        total = pred_piece(0, p)
+        for step in range(1, rows):
+            pred_copy(step, p).wait_recv()
+            total = total + pred_in[step - 1, :, p * part_cols:(p + 1) * part_cols].astype(f32)
+        out[:, p * part_cols:(p + 1) * part_cols] = total
 
     grad.drain()
     inner.drain()
@@ -557,7 +570,8 @@
         for step in range(1, second):
             second_copy(m, step).wait_send()
     for step in range(1, rows):
-        pred_copy(step).wait_send()
+        for p in range(parts):
+            pred_copy(step, p).wait_send()
 
 
 def per_device(mesh_shape, query_act, query_grad, train_rot, basis_in, basis_out, eig_in, eig_out):
@@ -575,7 +589,8 @@
     held = min(grad_held, num_grad)
     passes = inner_passes if num_act % inner_passes == 0 else 1
     group = 2 * (depth_in // depth_out)
-    cfg = dict(group=group, passes=passes, inner_held=min(inner_held, num_grad), split=(first, second), held=held, rows=rows, cols=cols, counts=(num_grad, num_act), width=width, act_width=act_width, wire=wire,
+    cut = pred_parts if depth_out % (128 * pred_parts) == 0 else 1
+    cfg = dict(pred_parts=cut, group=group, passes=passes, inner_held=min(inner_held, num_grad), split=(first, second), held=held, rows=rows, cols=cols, counts=(num_grad, num_act), width=width, act_width=act_width, wire=wire,
                factor=1.0 / float(eig_in.shape[0]) ** 0.5, block=min(512, in_cols // passes))
     dma = pltpu.SemaphoreType.DMA
     half_q, half_t = queries // 2, trains // 2
@@ -610,7 +625,7 @@
            dma((2, max(second - 1, 1))), dma((num_act, max(second - 1, 1))),
            dma((num_act, first - 1, second)), dma((num_act, first - 1, second)),
            dma((num_act, max(second - 1, 1))), dma((num_act, max(second - 1, 1))),
-           dma((rows - 1,)), dma((rows - 1,))]
+           dma((rows - 1, cut)), dma((rows - 1, cut))]
     )
     hbm = pl.BlockSpec(memory_space=pl.ANY)
     vmem = pl.BlockSpec(memory_space=pltpu.VMEM)

time: 165 us -> 162 us (0.982)
  Pallas kernels: 163 us -> 159 us
    pallas_call x1, Pallas kernels: 163 us -> 159 us  [per_device(): pl.pallas_call(functools.partial(kernel, cfg), out_shape=jax.ShapeDtypeSt...]
where the time goes in v2:
time: 162 us; the launch traced here: 161 us
  Pallas kernels  159 us (98%)
  local copies, waits for them, and re-layouts  2.06 us (1%)
    pallas_call x1, Pallas kernels, per_device(): pl.pallas_call(functools.partial(kernel, cfg), out_shape=jax.ShapeDtypeSt...  159 us

profile of v2, /device:TPU:0, one launch (start us, length us, event | category | flops | bytes accessed | tf_op | source)
XLA Modules:
  0.0 161.5 jit_solution(9158896656135428473)
XLA Ops:
  0.0 159.4 %shard_map.73 = f32[96,2048]{1,0:T(8,128)} custom-call(bf16[768,4096]{1,0:T(8,128)(2,1)} %qa.1, bf16[768,2048]{1,0:T(8,128)(2,1)} %qg.1, bf16[384,2048]{1,0:T(8,128)(2,1)} %tr.1, bf16[4096,2048]{1,0:T(8,128)(2,1)} %bi.1, bf16[2048,4096]{1,0:T(8,128)(2,1)} %bo.1, f32[1,16384]{1,0:T(1,128)} %bitcast.2, f32[1,16384]{1,0:T(1,128)} %bitcast.3), custom_call_target="tpu_custom_call" | custom-call | tf_op jit(solution)/shard_map/pallas_call | solution.py:632
  159.4 2.1 %copy.9 = f32[96,2048]{1,0:T(8,128)} copy(f32[96,2048]{1,0:T(8,128)} %shard_map.73) | data formatting | bytes 1572864

commit v3 on v2

--- a/solution.py
+++ b/solution.py
@@ -204,10 +204,10 @@
     grad_bufs, inner_bufs = take(8), take(8)
     (qa_v, qg_v, tr_v, wide_v, bo_v, ei_b, eo_q, scaled_v,
      act_part, act_own, act_out, act_out2, act_in, act_in2, act_full, act_t,
-     pred, pred_out, pred_in, damp_s) = take(20)
+     pred, pred_out, pred_in, pred_out2, pred_in2, damp_s) = take(22)
     grad_sems, inner_sems = take(9), take(9)
     (load_s, bi_s, bo_s, group_s, act_os, act_or, act_os2, act_or2, gat_s, gat_r, gat_s2, gat_r2,
-     pred_s, pred_r) = take(14)
+     pred_s, pred_r, pred_s2, pred_r2) = take(16)
 
     me = lax.axis_index("row")
     col = lax.axis_index("col")
@@ -537,30 +537,52 @@
 
     lax.fori_loop(0, steps, timestep, 0)
 
-    def pred_copy(step, p):
-        at_cols = slice(p * part_cols, (p + 1) * part_cols)
-        return remote(pred_out.at[step - 1, :, at_cols], pred_in.at[step - 1, :, at_cols], pred_s.at[step - 1, p],
-                      pred_r.at[step - 1, p], {"row": peer(step)})
-
-    def pred_piece(step, p):
-        return pred[pl.ds(pl.multiple_of(peer(step) * piece_t, 8), piece_t), p * part_cols:(p + 1) * part_cols]
-
     parts = cfg["pred_parts"]
     part_cols = depth_out // parts
+
+    def cols_of(p):
+        return slice(p * part_cols, (p + 1) * part_cols)
+
+    def rows_of(r):
+        return pl.ds(pl.multiple_of(r * piece_t, 8), piece_t)
+
+    def pred_first(p, step):
+        u, v, row = axes(p)
+        return remote(pred_out.at[p, step - 1], pred_in.at[p, step - 1], pred_s.at[p, step - 1],
+                      pred_r.at[p, step - 1], {"row": row((u + step) % first, v)})
+
+    def pred_second(p, step):
+        u, v, row = axes(p)
+        return remote(pred_out2.at[p, step - 1], pred_in2.at[p, step - 1], pred_s2.at[p, step - 1],
+                      pred_r2.at[p, step - 1], {"row": row(u, (v + step) % second)})
+
     last = pred_operand(num_groups - 1)
     for p in range(parts):
-        here = slice(p * part_cols, (p + 1) * part_cols)
+        here = cols_of(p)
+        u, v, row = axes(p)
         term = pred_term(last, wide_v[here, :])
         pred[:, here] = term if num_groups == 1 else pred[:, here] + term
-        for step in range(1, rows):
-            pred_out[step - 1, :, here] = pred_piece(step, p).astype(bf16)
-            pred_copy(step, p).start()
+        for step in range(1, first):
+            for j in range(second):
+                pred_out[p, step - 1, j] = pred[rows_of(row((u + step) % first, j)), here].astype(bf16)
+            pred_first(p, step).start()
     for p in range(parts):
-        total = pred_piece(0, p)
-        for step in range(1, rows):
-            pred_copy(step, p).wait_recv()
-            total = total + pred_in[step - 1, :, p * part_cols:(p + 1) * part_cols].astype(f32)
-        out[:, p * part_cols:(p + 1) * part_cols] = total
+        here = cols_of(p)
+        u, v, row = axes(p)
+        for step in range(1, first):
+            pred_first(p, step).wait_recv()
+            for j in range(second):
+                pred[rows_of(row(u, j)), here] += pred_in[p, step - 1, j].astype(f32)
+        for step in range(1, second):
+            pred_out2[p, step - 1] = pred[rows_of(row(u, (v + step) % second)), here].astype(bf16)
+            pred_second(p, step).start()
+    for p in range(parts):
+        here = cols_of(p)
+        total = pred[rows_of(me), here]
+        for step in range(1, second):
+            pred_second(p, step).wait_recv()
+            total = total + pred_in2[p, step - 1].astype(f32)
+        out[:, here] = total
 
     grad.drain()
     inner.drain()
@@ -569,9 +591,11 @@
             first_copy(m, step).wait_send()
         for step in range(1, second):
             second_copy(m, step).wait_send()
-    for step in range(1, rows):
-        for p in range(parts):
-            pred_copy(step, p).wait_send()
+    for p in range(parts):
+        for step in range(1, first):
+            pred_first(p, step).wait_send()
+        for step in range(1, second):
+            pred_second(p, step).wait_send()
 
 
 def per_device(mesh_shape, query_act, query_grad, train_rot, basis_in, basis_out, eig_in, eig_out):
@@ -616,8 +640,10 @@
             pltpu.VMEM((num_act, rows, piece_q, act_width), bf16),
             pltpu.VMEM((in_cols, queries), bf16),
             pltpu.VMEM((trains, depth_out), f32),
-            pltpu.VMEM((rows - 1, piece_t, depth_out), bf16),
-            pltpu.VMEM((rows - 1, piece_t, depth_out), bf16),
+            pltpu.VMEM((cut, first - 1, second, piece_t, depth_out // cut), bf16),
+            pltpu.VMEM((cut, first - 1, second, piece_t, depth_out // cut), bf16),
+            pltpu.VMEM((cut, max(second - 1, 1), piece_t, depth_out // cut), bf16),
+            pltpu.VMEM((cut, max(second - 1, 1), piece_t, depth_out // cut), bf16),
             pltpu.SMEM((1,), f32),
         ]
         + Line.semaphores(num_grad, 2) + Line.semaphores(num_grad, inner_pairs)
@@ -625,7 +651,8 @@
            dma((2, max(second - 1, 1))), dma((num_act, max(second - 1, 1))),
            dma((num_act, first - 1, second)), dma((num_act, first - 1, second)),
            dma((num_act, max(second - 1, 1))), dma((num_act, max(second - 1, 1))),
-           dma((rows - 1, cut)), dma((rows - 1, cut))]
+           dma((cut, first - 1)), dma((cut, first - 1)),
+           dma((cut, max(second - 1, 1))), dma((cut, max(second - 1, 1)))]
     )
     hbm = pl.BlockSpec(memory_space=pl.ANY)
     vmem = pl.BlockSpec(memory_space=pltpu.VMEM)

time: 162 us -> 159 us (0.981)
  Pallas kernels: 159 us -> 156 us
    pallas_call x1, Pallas kernels: 159 us -> 156 us  [per_device(): pl.pallas_call(functools.partial(kernel, cfg), out_shape=jax.ShapeDtypeSt...]
where the time goes in v3:
time: 159 us; the launch traced here: 158 us
  Pallas kernels  156 us (98%)
  local copies, waits for them, and re-layouts  2.06 us (1%)
    pallas_call x1, Pallas kernels, per_device(): pl.pallas_call(functools.partial(kernel, cfg), out_shape=jax.ShapeDtypeSt...  156 us

profile of v3, /device:TPU:0, one launch (start us, length us, event | category | flops | bytes accessed | tf_op | source)
XLA Modules:
  0.0 158.4 jit_solution(12048388524656930534)
XLA Ops:
  0.0 156.4 %shard_map.73 = f32[96,2048]{1,0:T(8,128)} custom-call(bf16[768,4096]{1,0:T(8,128)(2,1)} %qa.1, bf16[768,2048]{1,0:T(8,128)(2,1)} %qg.1, bf16[384,2048]{1,0:T(8,128)(2,1)} %tr.1, bf16[4096,2048]{1,0:T(8,128)(2,1)} %bi.1, bf16[2048,4096]{1,0:T(8,128)(2,1)} %bo.1, f32[1,16384]{1,0:T(1,128)} %bitcast.2, f32[1,16384]{1,0:T(1,128)} %bitcast.3), custom_call_target="tpu_custom_call" | custom-call | tf_op jit(solution)/shard_map/pallas_call | solution.py:659
  156.4 2.1 %copy.9 = f32[96,2048]{1,0:T(8,128)} copy(f32[96,2048]{1,0:T(8,128)} %shard_map.73) | data formatting | bytes 1572864

commit v4 on v3

--- a/solution.py
+++ b/solution.py
@@ -15,7 +15,7 @@
 grad_slots = 4
 grad_held = 6
 inner_held = 8
-pred_parts = 4
+pred_parts = 8
 inner_pairs = 4
 inner_pair_lag = 2
 inner_passes = 2

time: 159 us -> 159 us (level)
  no operation moved by 1% of the time
where the time goes in v4:
time: 159 us; the launch traced here: 158 us
  Pallas kernels  156 us (98%)
  local copies, waits for them, and re-layouts  2.06 us (1%)
    pallas_call x1, Pallas kernels, per_device(): pl.pallas_call(functools.partial(kernel, cfg), out_shape=jax.ShapeDtypeSt...  156 us

profile of v4, /device:TPU:0, one launch (start us, length us, event | category | flops | bytes accessed | tf_op | source)
XLA Modules:
  0.0 158.5 jit_solution(4682379028361339285)
XLA Ops:
  0.0 156.4 %shard_map.73 = f32[96,2048]{1,0:T(8,128)} custom-call(bf16[768,4096]{1,0:T(8,128)(2,1)} %qa.1, bf16[768,2048]{1,0:T(8,128)(2,1)} %qg.1, bf16[384,2048]{1,0:T(8,128)(2,1)} %tr.1, bf16[4096,2048]{1,0:T(8,128)(2,1)} %bi.1, bf16[2048,4096]{1,0:T(8,128)(2,1)} %bo.1, f32[1,16384]{1,0:T(1,128)} %bitcast.2, f32[1,16384]{1,0:T(1,128)} %bitcast.3), custom_call_target="tpu_custom_call" | custom-call | tf_op jit(solution)/shard_map/pallas_call | solution.py:659
  156.4 2.1 %copy.9 = f32[96,2048]{1,0:T(8,128)} copy(f32[96,2048]{1,0:T(8,128)} %shard_map.73) | data formatting | bytes 1572864
